TPU v7x, 256 devices: a whole 4x4x8 slice. The times are simulated.
256 devices in a mesh: scen: 16 (over z, core), clus: 16 (over y, x).
Axes of the slice: x: 4, y: 4, z: 8, core: 2. Of those that a mesh axis runs over, the one named last changes fastest.
Arguments:
- duals: bfloat16 [16384, 2, 128], P(('scen', 'clus')), may hold values from -6 to 6
- blocks: bfloat16 [16384, 2, 128, 128], P(('scen', 'clus')), may hold values from -0.5 to 0.5
- prob: float32 [16384], P(('scen', 'clus')), may hold values from 0.25 to 4
- cluster_map: int32 [16384], P(('scen', 'clus')), may hold values from 0 to 15
- block_cols: int32 [16384, 2], P(('scen', 'clus')), may hold values from 0 to 255
- counts: int32 [256], P(('scen', 'clus')), may hold values from 16 to 64, as said below
- cut_owner_rows: int32 [256], replicated, may hold values from 0 to 255, as said below
Outputs:
- master_cuts: float32 [256, 32768], P('clus', 'scen')
Inputs may be any that keep to these rules, and one draw needn't show every extreme that they name: counts of live slots, one device holding 64 live slots in every draw. A permutation of the master cut rows; of the cuts k = i * 16 to (i + 1) * 16 - 1 at most 1 have cut_owner_rows[k] in e * 16 to (e + 1) * 16 - 1, for any i and e, and 1 is reached.
All inputs are finite; a program needn't handle non-finite values.
Results may differ from a plain program's by a relative error of at most 0.0029.
Values sent between devices are 32-bit elements; how exact they have to be, the bound alone decides.
A program may use at most 64 MiB of HBM per device.

v0:
```python
import jax
import jax.numpy as jnp
from jax import lax
from jax.sharding import PartitionSpec as P

N1 = 32768
KC = 16


def body(duals, blocks, prob, cluster_map, block_cols, counts, cut_owner_rows):
    slots = prob.shape[0]
    width = blocks.shape[-1]
    col_blocks = N1 // width
    cluster_position = lax.axis_index("clus")
    own_blocks = col_blocks // lax.axis_size("scen")
    columns = own_blocks * width
    live = jnp.arange(slots, dtype=jnp.int32) < counts[0]
    weight = jnp.where(live, prob, jnp.float32(0.0))
    weighted_duals = (weight[:, None, None] * duals.astype(jnp.float32)).astype(jnp.bfloat16)
    dual_products = jnp.einsum(
        "plqv,plq->plv", blocks, weighted_duals, preferred_element_type=jnp.float32
    )
    dual_products = dual_products.reshape(-1, width)
    keys = (cluster_map[:, None] * col_blocks + block_cols).reshape(-1)
    clus_part = keys // col_blocks
    col_part = keys % col_blocks
    valid = (col_part >= 0) & (col_part < lax.axis_size("scen") * own_blocks)
    target = jnp.where(valid, col_part * KC + clus_part, -1)
    onehot = (
        target[None, :]
        == jnp.arange(lax.axis_size("scen") * own_blocks * KC, dtype=jnp.int32)[:, None]
    ).astype(jnp.float32)
    summed = jnp.dot(
        onehot, dual_products, precision=lax.Precision.HIGHEST, preferred_element_type=jnp.float32
    )
    probability_shares = lax.psum_scatter(
        summed.reshape(lax.axis_size("scen") * own_blocks, KC, width),
        "scen",
        scatter_dimension=0,
        tiled=True,
    )
    reduced = jnp.transpose(probability_shares, (1, 0, 2)).reshape(KC, columns)
    owners = cut_owner_rows - cluster_position * KC
    onehot = (owners[None, :] == jnp.arange(KC, dtype=jnp.int32)[:, None]).astype(jnp.float32)
    return jnp.dot(
        onehot,
        lax.all_gather(reduced, "clus", axis=0, tiled=True),
        precision=lax.Precision.HIGHEST,
        preferred_element_type=jnp.float32,
    )


def solution(mesh):
    placed = (
        P(("scen", "clus"), None, None),
        P(("scen", "clus"), None, None, None),
        P(("scen", "clus")),
        P(("scen", "clus")),
        P(("scen", "clus"), None),
        P(("scen", "clus")),
        P(),
    )
    return jax.shard_map(
        body, mesh=mesh, in_specs=placed, out_specs=P("clus", "scen"), check_vma=False
    )
```

profile of v0, /device:TPU:1, one launch (start us, length us, event | category | flops | bytes accessed | tf_op | source)
XLA Modules:
  0.0 139.5 jit_solution(1167170672462910426)
XLA Ops:
  6.5 0.0 reduce-scatter.2.cloned.1.call-start
  7.2 0.7 broadcast_multiply_fusion
  7.9 0.7 broadcast_add_fusion
  8.5 0.1 copy.9
  8.6 0.1 reshape.86
  8.8 0.7 compare_select_fusion
  9.5 0.9 fusion.6
  10.3 3.4 %fusion.4 = f32[64,2,1,128]{3,2,1,0:T(1,128)S(1)} fusion(bf16[64,2,128,128]{3,2,1,0:T(8,128)(2,1)} %param.8, bf16[64,2,128,1]{2,1,0,3:T(2,128)(2,1)S(1)} %fusion.6), kind=kOutput, calls=%fused_computation.5 | convolution fusion | flops 4194304 | bytes 4292608 | tf_op jit(solution)/shard_map/plqv,plq->plv/dot_general | solution.py:20
  13.7 0.0 copy-start
  13.7 2.5 %fusion = f32[256,16,128]{2,0,1:T(8,128)} fusion(f32[128,128,1]{1,0,2:T(8,128)S(1)} %bitcast.19, s32[256,16]{0,1:T(8,128)S(1)} %multiply_add_fusion, s32[128]{0:T(128)S(1)} %and_select_fusion.1), kind=kOutput, calls=%fused_computation | convolution fusion | flops 805830656 | bytes 2179584 | tf_op jit(solution)/shard_map/dot_general | solution.py:33
  16.2 0.0 reduce-scatter.2.cloned.1.call-update
  16.3 0.0 all-gather.2.cloned.1.call-start
  16.3 60.2 %reduce-scatter.2.cloned.1.call-done = f32[16,16,128]{2,0,1:T(8,128)} async-done(((f32[256,16,128]{2,0,1:T(8,128)}), f32[16,16,128]{2,0,1:T(8,128)}) %reduce-scatter.2.cloned.1.call-update) | async-done | bytes 131088 | tf_op jit(solution)/shard_map/reduce_scatter | solution.py:36
  76.6 1.6 %copy.16 = f32[2,8,16,128]{3,1,2,0:T(8,128)} copy(f32[2,8,16,128]{3,2,1,0:T(8,128)} %bitcast.20) | data formatting | bytes 262144
  78.2 0.0 all-gather.2.cloned.1.call-update
  78.2 0.0 copy-done
  78.2 51.4 %all-gather.2.cloned.1.call-done = f32[256,2048]{1,0:T(8,128)} async-done(((f32[16,2048]{1,0:T(8,128)}), f32[256,2048]{1,0:T(8,128)}) %all-gather.2.cloned.1.call-update) | async-done | bytes 2097168 | tf_op jit(solution)/shard_map/all_gather | solution.py:47
  129.6 3.0 %fusion.7 = f32[16,2048]{1,0:T(8,128)} fusion(f32[256,2048]{1,0:T(8,128)} %all-gather.2.cloned.1.call-done, s32[256]{0:T(256)S(1)} %broadcast_subtract_fusion), kind=kOutput, calls=%fused_computation.11 | convolution fusion | flops 100667392 | bytes 2229248 | tf_op jit(solution)/shard_map/dot_general | solution.py:45
  (3 shorter events, 0.0 us)
Async XLA Ops:
  6.5 70.0 %reduce-scatter.2.cloned.1.call-start = ((), (), s32[]{:S(2)}) async-start(), calls=%async_computation.1 | async-start | bytes 2228224 | tf_op jit(solution)/shard_map/reduce_scatter | solution.py:36
  13.7 64.5 %copy-start = (s32[256]{0:T(256)S(1)}, s32[256]{0:T(256)}, u32[]{:S(2)}) copy-start(s32[256]{0:T(256)} %param.13) | copy-start | bytes 3076
  16.3 113.3 %all-gather.2.cloned.1.call-start = ((), (), s32[]{:S(2)}) async-start(), calls=%async_computation.2 | async-start | bytes 2228224 | tf_op jit(solution)/shard_map/all_gather | solution.py:47
Sparse Core Ops, SparseCore 0:
  16.4 60.1 reduce-scatter.1
  79.0 50.5 all-gather.1
where the time goes:
time: 140 us; the launch traced here: 139 us
  waiting for transfers between devices  112 us (80%)
  between operations  14.1 us (10%)
  matrix products  8.91 us (6%)
  other arithmetic  2.91 us (2%)
  local copies, waits for them, and re-layouts  1.84 us (1%)
    reduce_scatter x1, waiting for transfers between devices, body(): lax.psum_scatter(summed.reshape(lax.axis_size('scen') * own_blocks, KC, w...  60.2 us
    all_gather x1, waiting for transfers between devices, body(): lax.all_gather(reduced, 'clus', axis=0, tiled=True)  51.4 us
    dot_general x1, matrix products, body(): jnp.einsum('plqv,plq->plv', blocks, weighted_duals, preferred_element_typ...  3.37 us
    dot_general x1, matrix products, body(): jnp.dot(onehot, lax.all_gather(reduced, 'clus', axis=0, tiled=True), prec...  3.02 us
  transfers between devices with their start and end apart: 2, of which 2 were waited for; matrix products, arithmetic and copies ran while one was open for 0% of the time, Pallas kernels for 0%

commit v1 on v0

--- a/solution.py
+++ b/solution.py
@@ -5,6 +5,25 @@
 
 N1 = 32768
 KC = 16
+
+
+def gather_around(x, axis, dim):
+    size, mine, rows = (lax.axis_size(axis), lax.axis_index(axis), x.shape[dim])
+    forward = [(i, (i + 1) % size) for i in range(size)]
+    backward = [(i, (i - 1) % size) for i in range(size)]
+    out = jnp.zeros((*x.shape[:dim], size * rows, *x.shape[dim + 1 :]), x.dtype)
+    out = lax.dynamic_update_slice_in_dim(out, x, mine * rows, axis=dim)
+    from_left = from_right = x
+    half = size // 2
+    for step in range(1, half + 1):
+        from_left = lax.ppermute(from_left, axis, forward)
+        out = lax.dynamic_update_slice_in_dim(out, from_left, (mine - step) % size * rows, axis=dim)
+        if step < size - half:
+            from_right = lax.ppermute(from_right, axis, backward)
+            out = lax.dynamic_update_slice_in_dim(
+                out, from_right, (mine + step) % size * rows, axis=dim
+            )
+    return out
 
 
 def body(duals, blocks, prob, cluster_map, block_cols, counts, cut_owner_rows):
@@ -44,7 +63,7 @@
     onehot = (owners[None, :] == jnp.arange(KC, dtype=jnp.int32)[:, None]).astype(jnp.float32)
     return jnp.dot(
         onehot,
-        lax.all_gather(reduced, "clus", axis=0, tiled=True),
+        gather_around(reduced, "clus", 0),
         precision=lax.Precision.HIGHEST,
         preferred_element_type=jnp.float32,
     )

time: 140 us -> 155 us (1.11)
  the two profiles are of different devices: /device:TPU:1 before, /device:TPU:0 now
where the time goes in v1:
time: 155 us; the launch traced here: 154 us
  waiting for transfers between devices  90.2 us (58%)
  starting transfers between devices  37.8 us (24%)
  between operations  14.5 us (9%)
  matrix products  7.28 us (5%)
  other arithmetic  2.92 us (2%)
  local copies, waits for them, and re-layouts  1.75 us (1%)
    reduce_scatter x1, waiting for transfers between devices, body(): lax.psum_scatter(summed.reshape(lax.axis_size('scen') * own_blocks, KC, w...  60.4 us
    ppermute x7, starting transfers between devices, gather_around(): from_right = lax.ppermute(from_right, axis, backward)  36.2 us
    ppermute x8, waiting for transfers between devices, gather_around(): from_left = lax.ppermute(from_left, axis, forward)  29.8 us
    dot_general x1, matrix products, body(): jnp.einsum('plqv,plq->plv', blocks, weighted_duals, preferred_element_typ...  3.37 us
  transfers between devices with their start and end apart: 16, of which 9 were waited for; matrix products, arithmetic and copies ran while one was open for 0% of the time, Pallas kernels for 0%

profile of v1, /device:TPU:0, one launch (start us, length us, event | category | flops | bytes accessed | tf_op | source)
XLA Modules:
  0.0 154.5 jit_solution(16136221652915514209)
XLA Ops:
  7.2 0.7 broadcast_multiply_fusion
  7.9 0.7 broadcast_add_fusion
  8.5 0.1 copy.9
  8.6 0.1 reshape.86
  8.8 0.7 compare_select_fusion
  9.5 0.9 fusion.6
  10.3 3.4 %fusion.4 = f32[64,2,1,128]{3,2,1,0:T(1,128)S(1)} fusion(bf16[64,2,128,128]{3,2,1,0:T(8,128)(2,1)} %param.8, bf16[64,2,128,1]{2,1,0,3:T(2,128)(2,1)S(1)} %fusion.6), kind=kOutput, calls=%fused_computation.5 | convolution fusion | flops 4194304 | bytes 4292608 | tf_op jit(solution)/shard_map/plqv,plq->plv/dot_general | solution.py:39
  13.7 2.5 %fusion = f32[256,16,128]{2,0,1:T(8,128)} fusion(f32[128,128,1]{1,0,2:T(8,128)S(1)} %bitcast.22, s32[256,16]{0,1:T(8,128)S(1)} %multiply_add_fusion, s32[128]{0:T(128)S(1)} %and_select_fusion.1), kind=kOutput, calls=%fused_computation | convolution fusion | flops 805830656 | bytes 2179584 | tf_op jit(solution)/shard_map/dot_general | solution.py:52
  16.2 0.0 reduce-scatter.2.cloned.1.call-update
  16.5 60.4 %reduce-scatter.2.cloned.1.call-done = f32[16,16,128]{2,0,1:T(8,128)} async-done(((f32[256,16,128]{2,0,1:T(8,128)}), f32[16,16,128]{2,0,1:T(8,128)}) %reduce-scatter.2.cloned.1.call-update) | async-done | bytes 131088 | tf_op jit(solution)/shard_map/reduce_scatter | solution.py:55
  76.9 1.0 copy.18
  77.9 1.6 %collective-permute-start = (f32[16,2048]{1,0:T(8,128)S(1)}, f32[16,2048]{1,0:T(8,128)S(1)}, u32[]{:S(2)}, u32[]{:S(2)}) collective-permute-start(f32[16,2048]{1,0:T(8,128)S(1)} %bitcast.23), channel_id=1, source_target_pairs={{0,1},{1,2},{2,3},{3,4},{4,5},{5,6},{6,7},{7,8},{8,9},{9,10},{10,1... | collective-permute-start | bytes 393224 | tf_op jit(solution)/shard_map/ppermute | solution.py:19
  79.5 3.9 %collective-permute-start.1 = (f32[16,2048]{1,0:T(8,128)S(1)}, f32[16,2048]{1,0:T(8,128)S(1)}, u32[]{:S(2)}, u32[]{:S(2)}) collective-permute-start(f32[16,2048]{1,0:T(8,128)S(1)} %bitcast.24), channel_id=1, source_target_pairs={{0,15},{1,0},{2,1},{3,2},{4,3},{5,4},{6,5},{7,6},{8,7},{9,8},{10,9... | collective-permute-start | bytes 393224 | tf_op jit(solution)/shard_map/ppermute | solution.py:22
  83.4 0.2 broadcast_in_dim.8
  83.7 2.6 %collective-permute-done = f32[16,2048]{1,0:T(8,128)S(1)} collective-permute-done((f32[16,2048]{1,0:T(8,128)S(1)}, f32[16,2048]{1,0:T(8,128)S(1)}, u32[]{:S(2)}, u32[]{:S(2)}) %collective-permute-start) | collective-permute-done | bytes 131104 | tf_op jit(solution)/shard_map/ppermute | solution.py:19
  86.3 0.0 collective-permute-start.2
  86.3 0.0 collective-permute-done.1
  86.3 5.3 %collective-permute-start.3 = (f32[16,2048]{1,0:T(8,128)S(1)}, f32[16,2048]{1,0:T(8,128)S(1)}, u32[]{:S(2)}, u32[]{:S(2)}) collective-permute-start(f32[16,2048]{1,0:T(8,128)S(1)} %collective-permute-done.1), channel_id=1, source_target_pairs={{0,15},{1,0},{2,1},{3,2},{4,3},{5,4},{6,5},{7,6},{8,7},{9,8},{10,9... | collective-permute-start | bytes 393224 | tf_op jit(solution)/shard_map/ppermute | solution.py:22
  91.7 2.9 %collective-permute-done.2 = f32[16,2048]{1,0:T(8,128)S(1)} collective-permute-done((f32[16,2048]{1,0:T(8,128)S(1)}, f32[16,2048]{1,0:T(8,128)S(1)}, u32[]{:S(2)}, u32[]{:S(2)}) %collective-permute-start.2) | collective-permute-done | bytes 131104 | tf_op jit(solution)/shard_map/ppermute | solution.py:19
  94.6 0.0 collective-permute-start.4
  94.6 5.3 %collective-permute-start.5 = (f32[16,2048]{1,0:T(8,128)S(1)}, f32[16,2048]{1,0:T(8,128)S(1)}, u32[]{:S(2)}, u32[]{:S(2)}) collective-permute-start(f32[16,2048]{1,0:T(8,128)S(1)} %collective-permute-done.3), channel_id=1, source_target_pairs={{0,15},{1,0},{2,1},{3,2},{4,3},{5,4},{6,5},{7,6},{8,7},{9,8},{10,9... | collective-permute-start | bytes 393224 | tf_op jit(solution)/shard_map/ppermute | solution.py:22
  100.0 3.6 %collective-permute-done.4 = f32[16,2048]{1,0:T(8,128)S(1)} collective-permute-done((f32[16,2048]{1,0:T(8,128)S(1)}, f32[16,2048]{1,0:T(8,128)S(1)}, u32[]{:S(2)}, u32[]{:S(2)}) %collective-permute-start.4) | collective-permute-done | bytes 131104 | tf_op jit(solution)/shard_map/ppermute | solution.py:19
  103.6 5.7 %collective-permute-start.7 = (f32[16,2048]{1,0:T(8,128)S(1)}, f32[16,2048]{1,0:T(8,128)S(1)}, u32[]{:S(2)}, u32[]{:S(2)}) collective-permute-start(f32[16,2048]{1,0:T(8,128)S(1)} %collective-permute-done.5), channel_id=1, source_target_pairs={{0,15},{1,0},{2,1},{3,2},{4,3},{5,4},{6,5},{7,6},{8,7},{9,8},{10,9... | collective-permute-start | bytes 393224 | tf_op jit(solution)/shard_map/ppermute | solution.py:22
  109.3 3.5 %collective-permute-done.6 = f32[16,2048]{1,0:T(8,128)S(1)} collective-permute-done((f32[16,2048]{1,0:T(8,128)S(1)}, f32[16,2048]{1,0:T(8,128)S(1)}, u32[]{:S(2)}, u32[]{:S(2)}) %collective-permute-start.6) | collective-permute-done | bytes 131104 | tf_op jit(solution)/shard_map/ppermute | solution.py:19
  112.8 5.3 %collective-permute-start.9 = (f32[16,2048]{1,0:T(8,128)S(1)}, f32[16,2048]{1,0:T(8,128)S(1)}, u32[]{:S(2)}, u32[]{:S(2)}) collective-permute-start(f32[16,2048]{1,0:T(8,128)S(1)} %collective-permute-done.7), channel_id=1, source_target_pairs={{0,15},{1,0},{2,1},{3,2},{4,3},{5,4},{6,5},{7,6},{8,7},{9,8},{10,9... | collective-permute-start | bytes 393224 | tf_op jit(solution)/shard_map/ppermute | solution.py:22
  118.2 3.1 %collective-permute-done.8 = f32[16,2048]{1,0:T(8,128)S(1)} collective-permute-done((f32[16,2048]{1,0:T(8,128)S(1)}, f32[16,2048]{1,0:T(8,128)S(1)}, u32[]{:S(2)}, u32[]{:S(2)}) %collective-permute-start.8) | collective-permute-done | bytes 131104 | tf_op jit(solution)/shard_map/ppermute | solution.py:19
  121.3 5.3 %collective-permute-start.11 = (f32[16,2048]{1,0:T(8,128)S(1)}, f32[16,2048]{1,0:T(8,128)S(1)}, u32[]{:S(2)}, u32[]{:S(2)}) collective-permute-start(f32[16,2048]{1,0:T(8,128)S(1)} %collective-permute-done.9), channel_id=1, source_target_pairs={{0,15},{1,0},{2,1},{3,2},{4,3},{5,4},{6,5},{7,6},{8,7},{9,8},{10,9... | collective-permute-start | bytes 393224 | tf_op jit(solution)/shard_map/ppermute | solution.py:22
  126.7 2.9 %collective-permute-done.10 = f32[16,2048]{1,0:T(8,128)S(1)} collective-permute-done((f32[16,2048]{1,0:T(8,128)S(1)}, f32[16,2048]{1,0:T(8,128)S(1)}, u32[]{:S(2)}, u32[]{:S(2)}) %collective-permute-start.10) | collective-permute-done | bytes 131104 | tf_op jit(solution)/shard_map/ppermute | solution.py:19
  129.6 5.3 %collective-permute-start.13 = (f32[16,2048]{1,0:T(8,128)S(1)}, f32[16,2048]{1,0:T(8,128)S(1)}, u32[]{:S(2)}, u32[]{:S(2)}) collective-permute-start(f32[16,2048]{1,0:T(8,128)S(1)} %collective-permute-done.11), channel_id=1, source_target_pairs={{0,15},{1,0},{2,1},{3,2},{4,3},{5,4},{6,5},{7,6},{8,7},{9,8},{10,9... | collective-permute-start | bytes 393224 | tf_op jit(solution)/shard_map/ppermute | solution.py:22
  135.0 2.9 %collective-permute-done.12 = f32[16,2048]{1,0:T(8,128)S(1)} collective-permute-done((f32[16,2048]{1,0:T(8,128)S(1)}, f32[16,2048]{1,0:T(8,128)S(1)}, u32[]{:S(2)}, u32[]{:S(2)}) %collective-permute-start.12) | collective-permute-done | bytes 131104 | tf_op jit(solution)/shard_map/ppermute | solution.py:19
  137.9 8.2 %collective-permute-done.14 = f32[16,2048]{1,0:T(8,128)S(1)} collective-permute-done((f32[16,2048]{1,0:T(8,128)S(1)}, f32[16,2048]{1,0:T(8,128)S(1)}, u32[]{:S(2)}, u32[]{:S(2)}) %collective-permute-start.14) | collective-permute-done | bytes 131104 | tf_op jit(solution)/shard_map/ppermute | solution.py:19
  146.2 1.5 fusion.7
  (35 shorter events, 0.3 us)
Async XLA Ops:
  6.5 70.4 %reduce-scatter.2.cloned.1.call-start = ((), (), s32[]{:S(2)}) async-start(), calls=%async_computation.1 | async-start | bytes 2228224 | tf_op jit(solution)/shard_map/reduce_scatter | solution.py:55
  13.7 2.8 %copy-start.1 = (s32[256]{0:T(256)S(1)}, s32[256]{0:T(256)}, u32[]{:S(2)}) copy-start(s32[256]{0:T(256)} %param.13) | copy-start | bytes 3076
  76.9 6.7 %copy-start = (f32[16,16,128]{2,0,1:T(8,128)S(1)}, f32[16,16,128]{2,0,1:T(8,128)}, u32[]{:S(2)}) copy-start(f32[16,16,128]{2,0,1:T(8,128)} %reduce-scatter.2.cloned.1.call-done) | copy-start | bytes 393220
  77.9 8.4 %collective-permute-start = (f32[16,2048]{1,0:T(8,128)S(1)}, f32[16,2048]{1,0:T(8,128)S(1)}, u32[]{:S(2)}, u32[]{:S(2)}) collective-permute-start(f32[16,2048]{1,0:T(8,128)S(1)} %bitcast.23), channel_id=1, source_target_pairs={{0,1},{1,2},{2,3},{3,4},{4,5},{5,6},{6,7},{7,8},{8,9},{9,10},{10,1... | collective-permute-start | bytes 393224 | tf_op jit(solution)/shard_map/ppermute | solution.py:19
  79.5 6.8 %collective-permute-start.1 = (f32[16,2048]{1,0:T(8,128)S(1)}, f32[16,2048]{1,0:T(8,128)S(1)}, u32[]{:S(2)}, u32[]{:S(2)}) collective-permute-start(f32[16,2048]{1,0:T(8,128)S(1)} %bitcast.24), channel_id=1, source_target_pairs={{0,15},{1,0},{2,1},{3,2},{4,3},{5,4},{6,5},{7,6},{8,7},{9,8},{10,9... | collective-permute-start | bytes 393224 | tf_op jit(solution)/shard_map/ppermute | solution.py:22
  86.3 8.3 %collective-permute-start.2 = (f32[16,2048]{1,0:T(8,128)S(1)}, f32[16,2048]{1,0:T(8,128)S(1)}, u32[]{:S(2)}, u32[]{:S(2)}) collective-permute-start(f32[16,2048]{1,0:T(8,128)S(1)} %collective-permute-done), channel_id=1, source_target_pairs={{0,1},{1,2},{2,3},{3,4},{4,5},{5,6},{6,7},{7,8},{8,9},{9,10},{10,1... | collective-permute-start | bytes 393224 | tf_op jit(solution)/shard_map/ppermute | solution.py:19
  86.3 8.3 %collective-permute-start.3 = (f32[16,2048]{1,0:T(8,128)S(1)}, f32[16,2048]{1,0:T(8,128)S(1)}, u32[]{:S(2)}, u32[]{:S(2)}) collective-permute-start(f32[16,2048]{1,0:T(8,128)S(1)} %collective-permute-done.1), channel_id=1, source_target_pairs={{0,15},{1,0},{2,1},{3,2},{4,3},{5,4},{6,5},{7,6},{8,7},{9,8},{10,9... | collective-permute-start | bytes 393224 | tf_op jit(solution)/shard_map/ppermute | solution.py:22
  94.6 9.0 %collective-permute-start.4 = (f32[16,2048]{1,0:T(8,128)S(1)}, f32[16,2048]{1,0:T(8,128)S(1)}, u32[]{:S(2)}, u32[]{:S(2)}) collective-permute-start(f32[16,2048]{1,0:T(8,128)S(1)} %collective-permute-done.2), channel_id=1, source_target_pairs={{0,1},{1,2},{2,3},{3,4},{4,5},{5,6},{6,7},{7,8},{8,9},{9,10},{10,1... | collective-permute-start | bytes 393224 | tf_op jit(solution)/shard_map/ppermute | solution.py:19
  94.6 9.0 %collective-permute-start.5 = (f32[16,2048]{1,0:T(8,128)S(1)}, f32[16,2048]{1,0:T(8,128)S(1)}, u32[]{:S(2)}, u32[]{:S(2)}) collective-permute-start(f32[16,2048]{1,0:T(8,128)S(1)} %collective-permute-done.3), channel_id=1, source_target_pairs={{0,15},{1,0},{2,1},{3,2},{4,3},{5,4},{6,5},{7,6},{8,7},{9,8},{10,9... | collective-permute-start | bytes 393224 | tf_op jit(solution)/shard_map/ppermute | solution.py:22
  103.6 9.2 %collective-permute-start.6 = (f32[16,2048]{1,0:T(8,128)S(1)}, f32[16,2048]{1,0:T(8,128)S(1)}, u32[]{:S(2)}, u32[]{:S(2)}) collective-permute-start(f32[16,2048]{1,0:T(8,128)S(1)} %collective-permute-done.4), channel_id=1, source_target_pairs={{0,1},{1,2},{2,3},{3,4},{4,5},{5,6},{6,7},{7,8},{8,9},{9,10},{10,1... | collective-permute-start | bytes 393224 | tf_op jit(solution)/shard_map/ppermute | solution.py:19
  103.6 9.2 %collective-permute-start.7 = (f32[16,2048]{1,0:T(8,128)S(1)}, f32[16,2048]{1,0:T(8,128)S(1)}, u32[]{:S(2)}, u32[]{:S(2)}) collective-permute-start(f32[16,2048]{1,0:T(8,128)S(1)} %collective-permute-done.5), channel_id=1, source_target_pairs={{0,15},{1,0},{2,1},{3,2},{4,3},{5,4},{6,5},{7,6},{8,7},{9,8},{10,9... | collective-permute-start | bytes 393224 | tf_op jit(solution)/shard_map/ppermute | solution.py:22
  112.8 8.4 %collective-permute-start.8 = (f32[16,2048]{1,0:T(8,128)S(1)}, f32[16,2048]{1,0:T(8,128)S(1)}, u32[]{:S(2)}, u32[]{:S(2)}) collective-permute-start(f32[16,2048]{1,0:T(8,128)S(1)} %collective-permute-done.6), channel_id=1, source_target_pairs={{0,1},{1,2},{2,3},{3,4},{4,5},{5,6},{6,7},{7,8},{8,9},{9,10},{10,1... | collective-permute-start | bytes 393224 | tf_op jit(solution)/shard_map/ppermute | solution.py:19
  112.8 8.4 %collective-permute-start.9 = (f32[16,2048]{1,0:T(8,128)S(1)}, f32[16,2048]{1,0:T(8,128)S(1)}, u32[]{:S(2)}, u32[]{:S(2)}) collective-permute-start(f32[16,2048]{1,0:T(8,128)S(1)} %collective-permute-done.7), channel_id=1, source_target_pairs={{0,15},{1,0},{2,1},{3,2},{4,3},{5,4},{6,5},{7,6},{8,7},{9,8},{10,9... | collective-permute-start | bytes 393224 | tf_op jit(solution)/shard_map/ppermute | solution.py:22
  121.3 8.3 %collective-permute-start.10 = (f32[16,2048]{1,0:T(8,128)S(1)}, f32[16,2048]{1,0:T(8,128)S(1)}, u32[]{:S(2)}, u32[]{:S(2)}) collective-permute-start(f32[16,2048]{1,0:T(8,128)S(1)} %collective-permute-done.8), channel_id=1, source_target_pairs={{0,1},{1,2},{2,3},{3,4},{4,5},{5,6},{6,7},{7,8},{8,9},{9,10},{10,1... | collective-permute-start | bytes 393224 | tf_op jit(solution)/shard_map/ppermute | solution.py:19
  121.3 8.3 %collective-permute-start.11 = (f32[16,2048]{1,0:T(8,128)S(1)}, f32[16,2048]{1,0:T(8,128)S(1)}, u32[]{:S(2)}, u32[]{:S(2)}) collective-permute-start(f32[16,2048]{1,0:T(8,128)S(1)} %collective-permute-done.9), channel_id=1, source_target_pairs={{0,15},{1,0},{2,1},{3,2},{4,3},{5,4},{6,5},{7,6},{8,7},{9,8},{10,9... | collective-permute-start | bytes 393224 | tf_op jit(solution)/shard_map/ppermute | solution.py:22
  129.6 8.3 %collective-permute-start.12 = (f32[16,2048]{1,0:T(8,128)S(1)}, f32[16,2048]{1,0:T(8,128)S(1)}, u32[]{:S(2)}, u32[]{:S(2)}) collective-permute-start(f32[16,2048]{1,0:T(8,128)S(1)} %collective-permute-done.10), channel_id=1, source_target_pairs={{0,1},{1,2},{2,3},{3,4},{4,5},{5,6},{6,7},{7,8},{8,9},{9,10},{10,1... | collective-permute-start | bytes 393224 | tf_op jit(solution)/shard_map/ppermute | solution.py:19
  129.6 8.3 %collective-permute-start.13 = (f32[16,2048]{1,0:T(8,128)S(1)}, f32[16,2048]{1,0:T(8,128)S(1)}, u32[]{:S(2)}, u32[]{:S(2)}) collective-permute-start(f32[16,2048]{1,0:T(8,128)S(1)} %collective-permute-done.11), channel_id=1, source_target_pairs={{0,15},{1,0},{2,1},{3,2},{4,3},{5,4},{6,5},{7,6},{8,7},{9,8},{10,9... | collective-permute-start | bytes 393224 | tf_op jit(solution)/shard_map/ppermute | solution.py:22
  137.8 8.3 %collective-permute-start.14 = (f32[16,2048]{1,0:T(8,128)S(1)}, f32[16,2048]{1,0:T(8,128)S(1)}, u32[]{:S(2)}, u32[]{:S(2)}) collective-permute-start(f32[16,2048]{1,0:T(8,128)S(1)} %collective-permute-done.12), channel_id=1, source_target_pairs={{0,1},{1,2},{2,3},{3,4},{4,5},{5,6},{6,7},{7,8},{8,9},{9,10},{10,1... | collective-permute-start | bytes 393224 | tf_op jit(solution)/shard_map/ppermute | solution.py:19
Sparse Core Ops, SparseCore 0:
  16.3 60.5 reduce-scatter.1
